TPU v7x, 256 devices: a whole 4x4x8 slice. The times are simulated.
256 devices in a mesh: gx: 16 (over z_hi, y, core), gy: 16 (over z_lo, x).
Axes of the slice: x: 4, y: 4, z: 8 (z_hi: 2, z_lo: 4; z = z_hi * 4 + z_lo), core: 2. Of those that a mesh axis runs over, the one named last changes fastest.
Arguments:
- skip_input: bfloat16 [32, 64, 4096], P(None, 'gx', 'gy'), may hold values from -6 to 6
- w_encoder: bfloat16 [64, 864], replicated, may hold values from -0.625 to 0.625
- w_bottom: bfloat16 [128, 1728], P('gx'), may hold values from -0.3125 to 0.3125
- w_middle: bfloat16 [64, 5184], replicated, may hold values from -0.15625 to 0.15625
- w_upper: bfloat16 [32, 2592], replicated, may hold values from -0.21875 to 0.21875
- cotangent: bfloat16 [32, 64, 4096], P(None, 'gx', 'gy'), may hold values from -6 to 6
Outputs:
- features: bfloat16 [32, 64, 4096], P(None, 'gx', 'gy')
- grad_skip: bfloat16 [32, 64, 4096], P(None, 'gx', 'gy')
- grad_encoder: float32 [64, 864], replicated
- grad_bottom: float32 [128, 1728], P('gx')
- grad_middle: float32 [64, 5184], replicated
- grad_upper: float32 [32, 2592], replicated
All inputs are finite; a program needn't handle non-finite values.
Results may differ from a plain program's by a relative error of at most 0.017.
Values may be sent and summed in bfloat16 or wider, within the bound.
No kernel may reach another device: no remote copies, remote signals or barrier semaphores. Data moves between devices by JAX's collectives and lax.ppermute only.
A program may use at most 64 MiB of HBM per device.

v0:
```python
import math
import jax
import jax.numpy as jnp
from jax import lax
from jax.sharding import PartitionSpec as P

Z = 16


def extended_2(cells, sides, width):
    for axis, dim in sides:
        count = lax.axis_size(axis)
        ends = count - 1
        head = lax.slice_in_dim(cells, 0, width, axis=dim)
        tail = lax.slice_in_dim(cells, cells.shape[dim] - width, cells.shape[dim], axis=dim)
        cells = jnp.concatenate(
            [
                lax.ppermute(tail, axis, [(i, (i + 1) % count) for i in range(ends)]),
                cells,
                lax.ppermute(head, axis, [((i + 1) % count, i) for i in range(ends)]),
            ],
            axis=dim,
        )
    return cells


def z_shift(extended, z_step, z_depth):
    length = extended.shape[2]
    padded = jnp.pad(extended, ((0, 0), (0, 0), (1, 1)))
    shifted = padded[:, :, 1 + z_step : 1 + z_step + length]
    z_index = lax.broadcasted_iota(jnp.int32, (1, 1, length), 2) % z_depth + z_step
    inside = (z_index >= 0) & (z_index < z_depth)
    return jnp.where(inside, shifted, jnp.zeros_like(shifted))


def tap_piece(shifted_set, a, b, c, row_count, col_count, z_depth, flipped):
    x_off, y_off, z_off = (2 - a, 2 - b, 2 - c) if flipped else (a, b, c)
    source = shifted_set[z_off]
    tap_slice = source[
        :, x_off : x_off + row_count, y_off * z_depth : (y_off + col_count) * z_depth
    ]
    return tap_slice.reshape(source.shape[0], row_count * col_count * z_depth)


def conv_forward(extended, weight, row_count, col_count, z_depth):
    in_chan = extended.shape[0]
    shifted_set = [z_shift(extended, z_step, z_depth) for z_step in (-1, 0, 1)]
    total_sum = jnp.zeros((weight.shape[0], row_count * col_count * z_depth), jnp.float32)
    for a in range(3):
        for b in range(3):
            for c in range(3):
                tap_number = 9 * a + 3 * b + c
                total_sum = total_sum + jnp.dot(
                    weight[:, tap_number * in_chan : (tap_number + 1) * in_chan],
                    tap_piece(shifted_set, a, b, c, row_count, col_count, z_depth, False),
                    preferred_element_type=jnp.float32,
                )
    return total_sum


def conv_backward(extended, weight, row_count, col_count, z_depth):
    in_chan = weight.shape[1] // 27
    shifted_set = [z_shift(extended, z_step, z_depth) for z_step in (-1, 0, 1)]
    total_sum = jnp.zeros((in_chan, row_count * col_count * z_depth), jnp.float32)
    for a in range(3):
        for b in range(3):
            for c in range(3):
                tap_number = 9 * a + 3 * b + c
                total_sum = total_sum + lax.dot_general(
                    weight[:, tap_number * in_chan : (tap_number + 1) * in_chan],
                    tap_piece(shifted_set, a, b, c, row_count, col_count, z_depth, True),
                    (((0,), (0,)), ((), ())),
                    preferred_element_type=jnp.float32,
                )
    return total_sum


def weight_grad(extended, error_flat, row_count, col_count, z_depth):
    shifted_set = [z_shift(extended, z_step, z_depth) for z_step in (-1, 0, 1)]
    blocks = []
    for a in range(3):
        for b in range(3):
            for c in range(3):
                blocks.append(
                    lax.dot_general(
                        error_flat,
                        tap_piece(shifted_set, a, b, c, row_count, col_count, z_depth, False),
                        (((1,), (1,)), ((), ())),
                        preferred_element_type=jnp.float32,
                    )
                )
    return jnp.concatenate(blocks, axis=1)


def pool_mean(values, z_depth):
    channels, row_count, length = values.shape
    col_count = length // z_depth
    shaped = values.astype(jnp.float32).reshape(
        channels, row_count // 2, 2, col_count // 2, 2, z_depth // 2, 2
    )
    return shaped.mean(axis=(2, 4, 6)).reshape(
        channels, row_count // 2, col_count // 2 * (z_depth // 2)
    )


def block_sum(values, z_depth):
    channels, row_count, length = values.shape
    col_count = length // z_depth
    shaped = values.reshape(channels, row_count // 2, 2, col_count // 2, 2, z_depth // 2, 2)
    return shaped.sum(axis=(2, 4, 6)).reshape(
        channels, row_count // 2, col_count // 2 * (z_depth // 2)
    )


def upsample(values, z_depth):
    channels, row_count, length = values.shape
    col_count = length // z_depth
    shaped = values.reshape(channels, row_count, 1, col_count, 1, z_depth, 1)
    shaped = jnp.broadcast_to(shaped, (channels, row_count, 2, col_count, 2, z_depth, 2))
    return shaped.reshape(channels, 2 * row_count, 4 * col_count * z_depth)


def silu_slope(values):
    s_value = jax.nn.sigmoid(values)
    return s_value * (1.0 + values * (1.0 - s_value))


def spatial_halo(values, z_depth):
    widened = extended_2(values, (("gx", 1),), 1)
    return extended_2(widened, (("gy", 2),), z_depth)


def per_device(skip_input, w_encoder, w_bottom, w_middle, w_upper, cotangent):
    top_chan = skip_input.shape[0]
    rows_fine = skip_input.shape[1]
    cols_fine = skip_input.shape[2] // Z
    rows_mid, cols_mid, depth_mid = (rows_fine // 2, cols_fine // 2, Z // 2)
    rows_low, cols_low, depth_low = (rows_fine // 4, cols_fine // 4, Z // 4)
    cells_fine = rows_fine * cols_fine * Z * lax.axis_size("gx") * lax.axis_size("gy")
    scale_fine = 1.0 / math.sqrt(cells_fine)
    scale_mid = 1.0 / math.sqrt(cells_fine // 8)
    scale_low = 1.0 / math.sqrt(cells_fine // 64)
    pool_top = pool_mean(skip_input, Z).astype(jnp.bfloat16)
    ext_pool = spatial_halo(pool_top, depth_mid)
    pre_one = conv_forward(ext_pool, w_encoder, rows_mid, cols_mid, depth_mid)
    act_one = jax.nn.silu(pre_one).astype(jnp.bfloat16).reshape(-1, rows_mid, cols_mid * depth_mid)
    pool_mid = pool_mean(act_one, depth_mid).astype(jnp.bfloat16)
    col_ext = extended_2(pool_mid, (("gy", 2),), depth_low)
    whole_rows = lax.all_gather(col_ext, "gx", axis=1, tiled=True)
    ext_low = jnp.pad(whole_rows, ((0, 0), (1, 1), (0, 0)))
    rows_all = whole_rows.shape[1]
    pre_two = conv_forward(ext_low, w_bottom, rows_all, cols_low, depth_low)
    act_block = (
        jax.nn.silu(pre_two).astype(jnp.bfloat16).reshape(-1, rows_all, cols_low * depth_low)
    )
    act_two = lax.all_to_all(act_block, "gx", split_axis=1, concat_axis=0, tiled=True)
    cat_mid = jnp.concatenate([upsample(act_two, depth_low), act_one], axis=0)
    ext_mid = spatial_halo(cat_mid, depth_mid)
    pre_three = conv_forward(ext_mid, w_middle, rows_mid, cols_mid, depth_mid)
    act_three = (
        jax.nn.silu(pre_three).astype(jnp.bfloat16).reshape(-1, rows_mid, cols_mid * depth_mid)
    )
    cat_top = jnp.concatenate([upsample(act_three, depth_mid), skip_input], axis=0)
    ext_top = spatial_halo(cat_top, Z)
    pre_four = conv_forward(ext_top, w_upper, rows_fine, cols_fine, Z)
    features = (
        jax.nn.silu(pre_four).astype(jnp.bfloat16).reshape(top_chan, rows_fine, cols_fine * Z)
    )
    err_four = (cotangent.reshape(top_chan, -1).astype(jnp.float32) * silu_slope(pre_four)).astype(
        jnp.bfloat16
    )
    local_upper = weight_grad(ext_top, err_four, rows_fine, cols_fine, Z) * scale_fine
    grad_upper = lax.psum(local_upper, ("gx", "gy"))
    dcat_top = conv_backward(
        spatial_halo(err_four.reshape(top_chan, rows_fine, cols_fine * Z), Z),
        w_upper,
        rows_fine,
        cols_fine,
        Z,
    ).reshape(-1, rows_fine, cols_fine * Z)
    mid_chan = act_three.shape[0]
    err_three = (
        block_sum(dcat_top[:mid_chan], Z).reshape(mid_chan, -1) * silu_slope(pre_three)
    ).astype(jnp.bfloat16)
    local_middle = weight_grad(ext_mid, err_three, rows_mid, cols_mid, depth_mid) * scale_mid
    grad_middle = lax.psum(local_middle, ("gx", "gy"))
    dcat_mid = conv_backward(
        spatial_halo(err_three.reshape(mid_chan, rows_mid, cols_mid * depth_mid), depth_mid),
        w_middle,
        rows_mid,
        cols_mid,
        depth_mid,
    ).reshape(-1, rows_mid, cols_mid * depth_mid)
    low_chan = act_two.shape[0]
    dact_two = block_sum(dcat_mid[:low_chan], depth_mid)
    dact_block = lax.all_to_all(dact_two, "gx", split_axis=0, concat_axis=1, tiled=True)
    block_chan = dact_block.shape[0]
    err_two = (dact_block.reshape(block_chan, -1) * silu_slope(pre_two)).astype(jnp.bfloat16)
    part_bottom = weight_grad(ext_low, err_two, rows_all, cols_low, depth_low)
    err_grid = err_two.reshape(block_chan, rows_all, cols_low * depth_low)
    err_cols = extended_2(err_grid, (("gy", 2),), depth_low)
    err_ext = jnp.pad(err_cols, ((0, 0), (1, 1), (0, 0)))
    partial_sum = conv_backward(err_ext, w_bottom, rows_all, cols_low, depth_low).reshape(
        -1, rows_all, cols_low * depth_low
    )
    dpool_mid = lax.psum_scatter(
        partial_sum.astype(jnp.bfloat16), "gx", scatter_dimension=1, tiled=True
    ).astype(jnp.float32)
    grad_bottom = lax.psum((part_bottom * scale_low).astype(jnp.bfloat16), "gy").astype(jnp.float32)
    dact_one = dcat_mid[low_chan:] + upsample(dpool_mid, depth_low) / 8.0
    err_one = (dact_one.reshape(mid_chan, -1) * silu_slope(pre_one)).astype(jnp.bfloat16)
    local_encoder = weight_grad(ext_pool, err_one, rows_mid, cols_mid, depth_mid) * scale_mid
    grad_encoder = lax.psum(local_encoder, ("gx", "gy"))
    dpool_top = conv_backward(
        spatial_halo(err_one.reshape(mid_chan, rows_mid, cols_mid * depth_mid), depth_mid),
        w_encoder,
        rows_mid,
        cols_mid,
        depth_mid,
    ).reshape(-1, rows_mid, cols_mid * depth_mid)
    grad_skip = (dcat_top[mid_chan:] + upsample(dpool_top, depth_mid) / 8.0).astype(jnp.bfloat16)
    return (features, grad_skip, grad_encoder, grad_bottom, grad_middle, grad_upper)


def solution(mesh):
    in_specs = (P(None, "gx", "gy"), P(), P("gx", None), P(), P(), P(None, "gx", "gy"))
    out_specs = (P(None, "gx", "gy"), P(None, "gx", "gy"), P(), P("gx", None), P(), P())
    return jax.shard_map(
        per_device, mesh=mesh, in_specs=in_specs, out_specs=out_specs, check_vma=False
    )
```

profile of v0, /device:TPU:4, one launch (start us, length us, event | category | flops | bytes accessed | tf_op | source)
XLA Modules:
  0.0 701.9 jit_solution(12189707919216640930)
XLA Ops:
  12.8 2.0 collective-permute-done.1
  14.8 3.1 collective-permute-start.2
  17.9 2.7 collective-permute-start.3
  21.4 2.1 collective-permute-done.3
  34.1 5.8 collective-permute-start.4
  41.9 3.5 collective-permute-done.5
  45.4 33.5 %all_gather.3 = bf16[64,16,24]{0,2,1:T(8,128)(2,1)S(1)} all-gather(bf16[64,1,24]{0,2,1:T(8,128)(2,1)S(1)} %pad_maximum_fusion.21), channel_id=1, replica_groups=mesh['gx'=16,'gy'=16] {'gx'}, dimensions={1}, use_global_device_ids=true | all-gather | bytes 52224 | tf_op jit(solution)/shard_map/all_gather | solution.py:149
  86.0 6.4 all-to-all-start
  92.6 9.9 %all-to-all-done = bf16[8,16,16]{2,0,1:T(8,128)(2,1)S(1)} async-done(((bf16[8,16,16]{2,0,1:T(8,128)(2,1)}), bf16[8,16,16]{2,0,1:T(8,128)(2,1)S(1)}, u32[]{:S(2)}, u32[]{:S(2)}) %all-to-all-start) | async-done | bytes 4128 | tf_op jit(solution)/shard_map/all_to_all | solution.py:156
  102.8 2.0 collective-permute-start.6
  108.0 4.2 collective-permute-start.8
  114.2 3.7 collective-permute-done.9
  127.1 3.1 collective-permute-start.10
  131.5 2.7 collective-permute-done.11
  134.4 4.1 collective-permute-start.12
  138.4 2.1 collective-permute-start.13
  140.6 3.6 collective-permute-done.13
  157.6 3.4 collective-permute-start.14
  162.8 2.3 collective-permute-done.15
  165.3 4.1 collective-permute-start.16
  172.7 2.8 collective-permute-done.17
  209.4 3.1 collective-permute-start.18
  217.7 4.0 collective-permute-start.20
  225.4 2.7 collective-permute-done.21
  270.0 28.7 %all-to-all-start.1 = ((f32[16,1,128]{2,1,0:T(1,128)}), f32[16,1,128]{2,1,0:T(1,128)S(1)}, u32[]{:S(2)}, u32[]{:S(2)}) async-start(f32[16,1,128]{2,1,0:T(1,128)} %reshape.1246), calls=%async_computation.1 | async-start | bytes 16384 | tf_op jit(solution)/shard_map/all_to_all | solution.py:196
  300.3 8.3 %all-to-all-done.1 = f32[16,1,128]{2,1,0:T(1,128)S(1)} async-done(((f32[16,1,128]{2,1,0:T(1,128)}), f32[16,1,128]{2,1,0:T(1,128)S(1)}, u32[]{:S(2)}, u32[]{:S(2)}) %all-to-all-start.1) | async-done | bytes 8224 | tf_op jit(solution)/shard_map/all_to_all | solution.py:196
  314.0 4.3 collective-permute-start.22
  320.5 3.6 collective-permute-done.23
  335.1 70.2 %psum.29 = bf16[8,1728]{1,0:T(8,128)(2,1)S(1)} all-reduce(bf16[8,1728]{1,0:T(8,128)(2,1)S(1)} %multiply_convert_fusion.3), channel_id=1, replica_groups=mesh['gx'=16,'gy'=16] {'gy'}, use_global_device_ids=true, to_apply=%region_6.7 | all-reduce | flops 13824 | bytes 55296 | tf_op jit(solution)/shard_map/psum | solution.py:209
  416.1 4.2 collective-permute-start.27
  435.2 254.7 %all-reduce.13.cloned.1.call-done = (f32[64,864]{0,1:T(8,128)}, f32[64,5184]{1,0:T(8,128)}, f32[32,2592]{1,0:T(8,128)}) async-done(((f32[64,864]{0,1:T(8,128)}, f32[64,5184]{1,0:T(8,128)}, f32[32,2592]{1,0:T(8,128)}), (f32[64,864]{0,1:T(8,128)}, f32[64,5184]{1,0:T(8,128)}, f32[32,2592]{1,0:T(8,128)})) %all-reduce.13.cloned.1.call-update) | async-done | bytes 1880080 | tf_op jit(solution)/shard_map/psum | solution.py:213
  691.8 2.5 copy.159
  (1002 shorter events, 190.3 us)
Async XLA Ops:
  8.6 4.2 collective-permute-start
  10.4 4.4 collective-permute-start.1
  14.8 8.8 %collective-permute-start.2 = (bf16[32,4,8]{0,2,1:T(8,128)(2,1)S(1)}, bf16[32,4,8]{0,2,1:T(8,128)(2,1)S(1)}, u32[]{:S(2)}, u32[]{:S(2)}) collective-permute-start(bf16[32,4,8]{0,2,1:T(8,128)(2,1)S(1)} %get-tuple-element.241), channel_id=1, source_target_pairs={{0,1},{1,2},{2,3},{3,4},{4,5},{5,6},{6,7},{7,8},{8,9},{9,10},{10,1... | collective-permute-start | bytes 6152 | tf_op jit(solution)/shard_map/ppermute | solution.py:18
  17.9 5.5 collective-permute-start.3
  34.1 7.8 %collective-permute-start.4 = (bf16[64,1,4]{0,2,1:T(4,128)(2,1)S(1)}, bf16[64,1,4]{0,2,1:T(4,128)(2,1)S(1)}, u32[]{:S(2)}, u32[]{:S(2)}) collective-permute-start(bf16[64,1,4]{0,2,1:T(4,128)(2,1)S(1)} %get-tuple-element.309), channel_id=1, source_target_pairs={{0,1},{1,2},{2,3},{3,4},{4,5},{5,6},{6,7},{7,8},{8,9},{9,10},{10,1... | collective-permute-start | bytes 1544 | tf_op jit(solution)/shard_map/ppermute | solution.py:18
  40.0 5.5 collective-permute-start.5
  86.0 16.4 %all-to-all-start = ((bf16[8,16,16]{2,0,1:T(8,128)(2,1)}), bf16[8,16,16]{2,0,1:T(8,128)(2,1)S(1)}, u32[]{:S(2)}, u32[]{:S(2)}) async-start(bf16[8,16,16]{2,0,1:T(8,128)(2,1)} %copy.83), calls=%async_computation | async-start | bytes 65536 | tf_op jit(solution)/shard_map/all_to_all | solution.py:156
  102.8 3.3 collective-permute-start.6
  104.8 3.2 collective-permute-start.7
  108.0 6.1 collective-permute-start.8
  112.2 5.6 collective-permute-start.9
  127.1 4.5 collective-permute-start.10
  130.2 4.1 collective-permute-start.11
  134.4 6.2 collective-permute-start.12
  138.4 5.7 collective-permute-start.13
  157.6 5.1 collective-permute-start.14
  161.1 4.0 collective-permute-start.15
  165.3 7.4 %collective-permute-start.16 = (bf16[32,6,16]{2,1,0:T(8,128)(2,1)S(1)}, bf16[32,6,16]{2,1,0:T(8,128)(2,1)S(1)}, u32[]{:S(2)}, u32[]{:S(2)}) collective-permute-start(bf16[32,6,16]{2,1,0:T(8,128)(2,1)S(1)} %get-tuple-element.138), channel_id=1, source_target_pairs={{0,1},{1,2},{2,3},{3,4},{4,5},{5,6},{6,7},{7,8},{8,9},{9,10},{10,1... | collective-permute-start | bytes 18440 | tf_op jit(solution)/shard_map/ppermute | solution.py:18
  169.3 6.2 collective-permute-start.17
  209.4 5.4 collective-permute-start.18
  212.5 4.3 collective-permute-start.19
  217.7 7.8 %collective-permute-start.20 = (bf16[64,4,8]{2,1,0:T(4,128)(2,1)}, bf16[64,4,8]{2,1,0:T(4,128)(2,1)}, u32[]{:S(2)}, u32[]{:S(2)}) collective-permute-start(bf16[64,4,8]{2,1,0:T(4,128)(2,1)} %get-tuple-element.235), channel_id=1, source_target_pairs={{0,1},{1,2},{2,3},{3,4},{4,5},{5,6},{6,7},{7,8},{8,9},{9,10},{10,1... | collective-permute-start | bytes 12296 | tf_op jit(solution)/shard_map/ppermute | solution.py:18
  221.7 6.5 collective-permute-start.21
  270.0 38.6 %all-to-all-start.1 = ((f32[16,1,128]{2,1,0:T(1,128)}), f32[16,1,128]{2,1,0:T(1,128)S(1)}, u32[]{:S(2)}, u32[]{:S(2)}) async-start(f32[16,1,128]{2,1,0:T(1,128)} %reshape.1246), calls=%async_computation.1 | async-start | bytes 16384 | tf_op jit(solution)/shard_map/all_to_all | solution.py:196
  298.8 107.2 %reduce-scatter.2.cloned.1.call-start = ((), (), s32[]{:S(2)}) async-start(), calls=%async_computation.3 | async-start | bytes 69632 | tf_op jit(solution)/shard_map/reduce_scatter | solution.py:206
  314.0 6.5 collective-permute-start.22
  318.3 5.8 collective-permute-start.23
  335.0 354.9 %all-reduce.13.cloned.1.call-start = ((), (), s32[]{:S(2)}) async-start(), calls=%async_computation.4 | async-start | bytes 4259840 | tf_op jit(solution)/shard_map/psum | solution.py:213
  407.8 6.2 collective-permute-start.24
  409.1 4.9 collective-permute-start.25
  414.2 7.0 collective-permute-start.26
  416.1 6.2 collective-permute-start.27
  (176 other events, 3641.9 us)
Sparse Core Ops, SparseCore 0:
  335.1 68.1 reduce-scatter.1
  421.3 268.5 all-reduce.12
where the time goes:
time: 705 us; the launch traced here: 702 us
  waiting for transfers between devices  307 us (44%)
  starting transfers between devices  108 us (15%)
  blocking collectives  104 us (15%)
  matrix products  87.8 us (12%)
  local copies, waits for them, and re-layouts  58.3 us (8%)
  other arithmetic  19.2 us (3%)
  between operations  17.9 us (3%)
    psum x1, waiting for transfers between devices, per_device(): grad_encoder = lax.psum(local_encoder, ('gx', 'gy'))  255 us
    psum x1, blocking collectives, per_device(): lax.psum((part_bottom * scale_low).astype(jnp.bfloat16), 'gy')  70.2 us
    ppermute x14, starting transfers between devices, extended_2(): lax.ppermute(tail, axis, [(i, (i + 1) % count) for i in range(ends)])  46.2 us
    ppermute x14, waiting for transfers between devices, extended_2(): lax.ppermute(head, axis, [((i + 1) % count, i) for i in range(ends)])  34.1 us
    all_gather x1, blocking collectives, per_device(): whole_rows = lax.all_gather(col_ext, 'gx', axis=1, tiled=True)  33.5 us
    dot_general x108, matrix products, weight_grad(): lax.dot_general(error_flat, tap_piece(shifted_set, a, b, c, row_count, co...  33.3 us
    dot_general x108, matrix products, conv_backward(): lax.dot_general(weight[:, tap_number * in_chan:(tap_number + 1) * in_chan...  32.1 us
    reshape x108, local copies, waits for them, and re-layouts, tap_piece(): return tap_slice.reshape(source.shape[0], row_count * col_count * z_depth)  30.8 us
  transfers between devices with their start and end apart: 32, of which 16 were waited for; matrix products, arithmetic and copies ran while one was open for 4% of the time, Pallas kernels for 0%

commit v1 on v0

--- a/solution.py
+++ b/solution.py
@@ -5,6 +5,10 @@
 from jax.sharding import PartitionSpec as P
 
 Z = 16
+
+
+def lay_view(load):
+    return jnp.sum(lax.all_gather(load, "gy"), axis=0)
 
 
 def extended_2(cells, sides, width):
@@ -206,7 +210,7 @@
     dpool_mid = lax.psum_scatter(
         partial_sum.astype(jnp.bfloat16), "gx", scatter_dimension=1, tiled=True
     ).astype(jnp.float32)
-    grad_bottom = lax.psum((part_bottom * scale_low).astype(jnp.bfloat16), "gy").astype(jnp.float32)
+    grad_bottom = lay_view((part_bottom * scale_low).astype(jnp.bfloat16)).astype(jnp.float32)
     dact_one = dcat_mid[low_chan:] + upsample(dpool_mid, depth_low) / 8.0
     err_one = (dact_one.reshape(mid_chan, -1) * silu_slope(pre_one)).astype(jnp.bfloat16)
     local_encoder = weight_grad(ext_pool, err_one, rows_mid, cols_mid, depth_mid) * scale_mid

time: 705 us -> 703 us (level)
  blocking collectives: 104 us -> 68.8 us
  waiting for transfers between devices: 307 us -> 341 us
    psum x1 -> x0, blocking collectives: 70.2 us -> none  [per_device(): lax.psum((part_bottom * scale_low).astype(jnp.bfloat16), 'gy')]
    all_gather x0 -> x1, blocking collectives: none -> 35.2 us  [lay_view(): return jnp.sum(lax.all_gather(load, 'gy'), axis=0)]
    reduce_scatter x1, waiting for transfers between devices: 0.01 us -> 32.3 us  [per_device(): lax.psum_scatter(partial_sum.astype(jnp.bfloat16), 'gx', scatter_dimensio...]
  transfers between devices with their start and end apart: 32 -> 32, of which waited for: 16 -> 17; matrix products, arithmetic and copies ran while one was open for 4% -> 4% of each run, Pallas kernels for 0% -> 0%
where the time goes in v1:
time: 703 us; the launch traced here: 701 us
  waiting for transfers between devices  341 us (49%)
  starting transfers between devices  108 us (15%)
  matrix products  87.8 us (12%)
  blocking collectives  68.8 us (10%)
  local copies, waits for them, and re-layouts  58.3 us (8%)
  other arithmetic  19.3 us (3%)
  between operations  17.8 us (3%)
    psum x1, waiting for transfers between devices, per_device(): grad_encoder = lax.psum(local_encoder, ('gx', 'gy'))  255 us
    ppermute x14, starting transfers between devices, extended_2(): lax.ppermute(tail, axis, [(i, (i + 1) % count) for i in range(ends)])  47.3 us
    ppermute x14, waiting for transfers between devices, extended_2(): lax.ppermute(head, axis, [((i + 1) % count, i) for i in range(ends)])  35.3 us
    all_gather x1, blocking collectives, lay_view(): return jnp.sum(lax.all_gather(load, 'gy'), axis=0)  35.2 us
    all_gather x1, blocking collectives, per_device(): whole_rows = lax.all_gather(col_ext, 'gx', axis=1, tiled=True)  33.5 us
    dot_general x108, matrix products, weight_grad(): lax.dot_general(error_flat, tap_piece(shifted_set, a, b, c, row_count, co...  33.3 us
    reduce_scatter x1, waiting for transfers between devices, per_device(): lax.psum_scatter(partial_sum.astype(jnp.bfloat16), 'gx', scatter_dimensio...  32.3 us
    dot_general x108, matrix products, conv_backward(): lax.dot_general(weight[:, tap_number * in_chan:(tap_number + 1) * in_chan...  32.1 us
  transfers between devices with their start and end apart: 32, of which 17 were waited for; matrix products, arithmetic and copies ran while one was open for 4% of the time, Pallas kernels for 0%

profile of v1, /device:TPU:4, one launch (start us, length us, event | category | flops | bytes accessed | tf_op | source)
XLA Modules:
  0.0 700.5 jit_solution(5753229995095539862)
XLA Ops:
  14.8 3.1 collective-permute-start.2
  17.9 2.7 collective-permute-start.3
  21.4 2.1 collective-permute-done.3
  34.1 5.8 collective-permute-start.4
  41.9 3.5 collective-permute-done.5
  45.5 33.5 %all_gather.7 = bf16[64,16,24]{0,2,1:T(8,128)(2,1)S(1)} all-gather(bf16[64,1,24]{0,2,1:T(8,128)(2,1)S(1)} %pad_maximum_fusion.21), channel_id=1, replica_groups=mesh['gx'=16,'gy'=16] {'gx'}, dimensions={1}, use_global_device_ids=true | all-gather | bytes 52224 | tf_op jit(solution)/shard_map/all_gather | solution.py:153
  86.0 6.4 all-to-all-start
  92.6 9.9 %all-to-all-done = bf16[8,16,16]{2,0,1:T(8,128)(2,1)S(1)} async-done(((bf16[8,16,16]{2,0,1:T(8,128)(2,1)}), bf16[8,16,16]{2,0,1:T(8,128)(2,1)S(1)}, u32[]{:S(2)}, u32[]{:S(2)}) %all-to-all-start) | async-done | bytes 4128 | tf_op jit(solution)/shard_map/all_to_all | solution.py:160
  108.0 4.2 collective-permute-start.8
  114.2 3.7 collective-permute-done.9
  127.1 3.1 collective-permute-start.10
  131.5 2.7 collective-permute-done.11
  134.4 4.1 collective-permute-start.12
  140.6 3.6 collective-permute-done.13
  157.7 3.4 collective-permute-start.14
  162.8 2.3 collective-permute-done.15
  165.3 4.1 collective-permute-start.16
  172.7 2.8 collective-permute-done.17
  209.4 3.1 collective-permute-start.18
  217.7 4.0 collective-permute-start.20
  225.4 2.7 collective-permute-done.21
  270.0 28.7 %all-to-all-start.1 = ((f32[16,1,128]{2,1,0:T(1,128)}), f32[16,1,128]{2,1,0:T(1,128)S(1)}, u32[]{:S(2)}, u32[]{:S(2)}) async-start(f32[16,1,128]{2,1,0:T(1,128)} %reshape.1603), calls=%async_computation.1 | async-start | bytes 16384 | tf_op jit(solution)/shard_map/all_to_all | solution.py:200
  300.3 8.3 %all-to-all-done.1 = f32[16,1,128]{2,1,0:T(1,128)S(1)} async-done(((f32[16,1,128]{2,1,0:T(1,128)}), f32[16,1,128]{2,1,0:T(1,128)S(1)}, u32[]{:S(2)}, u32[]{:S(2)}) %all-to-all-start.1) | async-done | bytes 8224 | tf_op jit(solution)/shard_map/all_to_all | solution.py:200
  314.2 4.3 collective-permute-start.22
  320.5 3.8 collective-permute-done.23
  335.2 35.2 %all_gather.8 = bf16[16,8,1728]{2,1,0:T(8,128)(2,1)S(1)} all-gather(bf16[1,8,1728]{2,1,0:T(8,128)(2,1)S(1)} %multiply_convert_fusion.3), channel_id=1, replica_groups=mesh['gx'=16,'gy'=16] {'gy'}, dimensions={0}, use_global_device_ids=true | all-gather | bytes 470016 | tf_op jit(solution)/shard_map/all_gather | solution.py:11
  371.1 32.3 %reduce-scatter.2.cloned.1.call-done = bf16[64,1,16]{0,2,1:T(8,128)(2,1)} async-done(((bf16[64,16,16]{0,2,1:T(8,128)(2,1)}), bf16[64,1,16]{0,2,1:T(8,128)(2,1)}) %reduce-scatter.2.cloned.1.call-update) | async-done | bytes 2064 | tf_op jit(solution)/shard_map/reduce_scatter | solution.py:210
  411.7 3.1 collective-permute-start.26
  414.8 3.0 collective-permute-start.27
  418.7 2.3 collective-permute-done.27
  433.8 254.7 %all-reduce.13.cloned.1.call-done = (f32[64,864]{0,1:T(8,128)}, f32[64,5184]{1,0:T(8,128)}, f32[32,2592]{1,0:T(8,128)}) async-done(((f32[64,864]{0,1:T(8,128)}, f32[64,5184]{1,0:T(8,128)}, f32[32,2592]{1,0:T(8,128)}), (f32[64,864]{0,1:T(8,128)}, f32[64,5184]{1,0:T(8,128)}, f32[32,2592]{1,0:T(8,128)})) %all-reduce.13.cloned.1.call-update) | async-done | bytes 1880080 | tf_op jit(solution)/shard_map/psum | solution.py:217
  690.4 2.5 copy.159
  (1003 shorter events, 193.5 us)
Async XLA Ops:
  8.6 4.2 collective-permute-start
  10.4 4.4 collective-permute-start.1
  14.8 8.8 %collective-permute-start.2 = (bf16[32,4,8]{0,2,1:T(8,128)(2,1)S(1)}, bf16[32,4,8]{0,2,1:T(8,128)(2,1)S(1)}, u32[]{:S(2)}, u32[]{:S(2)}) collective-permute-start(bf16[32,4,8]{0,2,1:T(8,128)(2,1)S(1)} %get-tuple-element.241), channel_id=1, source_target_pairs={{0,1},{1,2},{2,3},{3,4},{4,5},{5,6},{6,7},{7,8},{8,9},{9,10},{10,1... | collective-permute-start | bytes 6152 | tf_op jit(solution)/shard_map/ppermute | solution.py:22
  17.9 5.5 collective-permute-start.3
  34.1 7.8 %collective-permute-start.4 = (bf16[64,1,4]{0,2,1:T(4,128)(2,1)S(1)}, bf16[64,1,4]{0,2,1:T(4,128)(2,1)S(1)}, u32[]{:S(2)}, u32[]{:S(2)}) collective-permute-start(bf16[64,1,4]{0,2,1:T(4,128)(2,1)S(1)} %get-tuple-element.309), channel_id=1, source_target_pairs={{0,1},{1,2},{2,3},{3,4},{4,5},{5,6},{6,7},{7,8},{8,9},{9,10},{10,1... | collective-permute-start | bytes 1544 | tf_op jit(solution)/shard_map/ppermute | solution.py:22
  40.0 5.5 collective-permute-start.5
  86.0 16.4 %all-to-all-start = ((bf16[8,16,16]{2,0,1:T(8,128)(2,1)}), bf16[8,16,16]{2,0,1:T(8,128)(2,1)S(1)}, u32[]{:S(2)}, u32[]{:S(2)}) async-start(bf16[8,16,16]{2,0,1:T(8,128)(2,1)} %copy.83), calls=%async_computation | async-start | bytes 65536 | tf_op jit(solution)/shard_map/all_to_all | solution.py:160
  102.8 3.3 collective-permute-start.6
  104.9 3.2 collective-permute-start.7
  108.0 6.1 collective-permute-start.8
  112.2 5.6 collective-permute-start.9
  127.1 4.5 collective-permute-start.10
  130.2 4.1 collective-permute-start.11
  134.4 6.2 collective-permute-start.12
  138.4 5.7 collective-permute-start.13
  157.7 5.1 collective-permute-start.14
  161.1 4.0 collective-permute-start.15
  165.3 7.4 %collective-permute-start.16 = (bf16[32,6,16]{2,1,0:T(8,128)(2,1)S(1)}, bf16[32,6,16]{2,1,0:T(8,128)(2,1)S(1)}, u32[]{:S(2)}, u32[]{:S(2)}) collective-permute-start(bf16[32,6,16]{2,1,0:T(8,128)(2,1)S(1)} %get-tuple-element.138), channel_id=1, source_target_pairs={{0,1},{1,2},{2,3},{3,4},{4,5},{5,6},{6,7},{7,8},{8,9},{9,10},{10,1... | collective-permute-start | bytes 18440 | tf_op jit(solution)/shard_map/ppermute | solution.py:22
  169.3 6.2 collective-permute-start.17
  209.4 5.4 collective-permute-start.18
  212.5 4.3 collective-permute-start.19
  217.7 7.8 %collective-permute-start.20 = (bf16[64,4,8]{2,1,0:T(4,128)(2,1)}, bf16[64,4,8]{2,1,0:T(4,128)(2,1)}, u32[]{:S(2)}, u32[]{:S(2)}) collective-permute-start(bf16[64,4,8]{2,1,0:T(4,128)(2,1)} %get-tuple-element.235), channel_id=1, source_target_pairs={{0,1},{1,2},{2,3},{3,4},{4,5},{5,6},{6,7},{7,8},{8,9},{9,10},{10,1... | collective-permute-start | bytes 12296 | tf_op jit(solution)/shard_map/ppermute | solution.py:22
  221.7 6.5 collective-permute-start.21
  270.0 38.6 %all-to-all-start.1 = ((f32[16,1,128]{2,1,0:T(1,128)}), f32[16,1,128]{2,1,0:T(1,128)S(1)}, u32[]{:S(2)}, u32[]{:S(2)}) async-start(f32[16,1,128]{2,1,0:T(1,128)} %reshape.1603), calls=%async_computation.1 | async-start | bytes 16384 | tf_op jit(solution)/shard_map/all_to_all | solution.py:200
  298.8 104.7 %reduce-scatter.2.cloned.1.call-start = ((), (), s32[]{:S(2)}) async-start(), calls=%async_computation.3 | async-start | bytes 69632 | tf_op jit(solution)/shard_map/reduce_scatter | solution.py:210
  314.2 6.4 collective-permute-start.22
  318.5 5.8 collective-permute-start.23
  335.1 353.4 %all-reduce.13.cloned.1.call-start = ((), (), s32[]{:S(2)}) async-start(), calls=%async_computation.4 | async-start | bytes 4259840 | tf_op jit(solution)/shard_map/psum | solution.py:217
  405.3 6.2 collective-permute-start.24
  406.6 4.9 collective-permute-start.25
  411.7 7.0 collective-permute-start.26
  414.8 6.2 collective-permute-start.27
  (176 other events, 3521.4 us)
Sparse Core Ops, SparseCore 0:
  335.3 68.1 reduce-scatter.1
  418.8 269.6 all-reduce.12
